TPU v7x, 128 devices: a whole 4x4x4 slice. The times are simulated.
128 devices in a mesh: rows: 8 (over z, core), cols: 16 (over x, y).
Axes of the slice: x: 4, y: 4, z: 4, core: 2. Of those that a mesh axis runs over, the one named last changes fastest.
Arguments:
- embeddings: bfloat16 [917504, 1024], P(('rows', 'cols'))
- factor_cols: bfloat16 [917504, 512], P(('rows', 'cols')), may hold values from -0.12 to 0.12, as said below
- solved: int32 [917504], P(('rows', 'cols')), may hold values from 0 to 16
- pivots: int32 [256], replicated, may hold values from 0 to 917503, as said below
Outputs:
- new_cols: bfloat16 [917504, 256], P(('rows', 'cols'))
- gains: float32 [917504], P(('rows', 'cols'))
- best_gain: float32 [], replicated
Inputs may be any that keep to these rules, and one draw needn't show every extreme that they name: `pivots`: 256 distinct row numbers in increasing order; the 7168 consecutive rows of one device hold at most 16 of them, and some device holds exactly 16. `factor_cols`: the pivots' factor rows F satisfy: every eigenvalue of F F^T is below 1.
All inputs are finite; a program needn't handle non-finite values.
Results may differ from a plain program's by a relative error of at most 0.001.
Values may be sent and summed in bfloat16 or wider, within the bound.
No kernel may reach another device: no remote copies, remote signals or barrier semaphores. Data moves between devices by JAX's collectives and lax.ppermute only.
A program may use at most 128 MiB of HBM per device.

v0:
```python
import jax
import jax.numpy as jnp
from jax import lax
from jax.sharding import PartitionSpec as P

PMAX = 16
EPS = 1e-06
TAU = 6.0
RIDGE = 1.0


def learn(counts):
    c = counts.astype(jnp.float32)
    return (c * (16.0 - c) + 8.0) / 72.0


def scales(emb):
    x = emb.astype(jnp.float32)
    return jnp.sqrt(jnp.mean(x * x, axis=1) + EPS)


def kernel_panel(
    left_emb, left_fac, left_q, left_norm, left_ids, piv_emb, piv_fac, piv_q, piv_norm, pivots
):
    dims = (((1,), (1,)), ((), ()))
    dots = lax.dot_general(left_emb, piv_emb, dims, preferred_element_type=jnp.float32)
    width = left_emb.shape[1] * 1.0
    cosine = dots / (width * left_norm[:, None] * piv_norm[None, :])
    similar = jnp.exp(TAU * (cosine - 1.0))
    ridge = jnp.where(left_ids[:, None] == pivots[None, :], RIDGE, 0.0)
    shared = lax.dot_general(left_fac, piv_fac, dims, preferred_element_type=jnp.float32)
    return left_q[:, None] * piv_q[None, :] * similar + ridge - shared


def body(embeddings, factor_cols, solved, pivots):
    rows_here = embeddings.shape[0]
    total = pivots.shape[0]
    device = lax.axis_index(("rows", "cols"))
    first_row = device * rows_here
    owner = pivots // rows_here
    before = jnp.sum((owner < device).astype(jnp.int32))
    mine = jnp.sum((owner == device).astype(jnp.int32))
    ranks = jnp.arange(PMAX, dtype=jnp.int32)
    valid = ranks < mine
    position = jnp.clip(before + ranks, 0, total - 1)
    local_idx = jnp.clip(pivots[position] - first_row, 0, rows_here - 1)
    keep = valid[:, None]
    own_emb = jnp.where(keep, embeddings[local_idx], 0)
    own_fac = jnp.where(keep, factor_cols[local_idx], 0)
    own_count = jnp.where(valid, solved[local_idx], 0).astype(jnp.bfloat16)
    place = (
        (jnp.arange(total, dtype=jnp.int32)[:, None] == (before + ranks)[None, :]) & valid[None, :]
    ).astype(jnp.float32)
    highest = lax.Precision.HIGHEST
    all_emb, all_fac, all_count = (
        lax.all_gather(own_emb, ("rows", "cols"), axis=0, tiled=True),
        lax.all_gather(own_fac, ("rows", "cols"), axis=0, tiled=True),
        lax.all_gather(own_count, ("rows", "cols"), axis=0, tiled=True),
    )
    earlier = jnp.sum((owner[None, :] < owner[:, None]).astype(jnp.int32), axis=1)
    slot_index = owner * PMAX + jnp.arange(total, dtype=jnp.int32) - earlier
    piv_emb = all_emb[slot_index]
    piv_fac = all_fac[slot_index]
    piv_count = all_count[slot_index].astype(jnp.float32)
    row_q = learn(solved)
    piv_q = learn(piv_count)
    piv_norm = scales(piv_emb)
    row_ids = first_row + jnp.arange(rows_here, dtype=jnp.int32)
    panel = kernel_panel(
        embeddings,
        factor_cols,
        row_q,
        scales(embeddings),
        row_ids,
        piv_emb,
        piv_fac,
        piv_q,
        piv_norm,
        pivots,
    )
    own_rows = jnp.where(keep, panel[local_idx], 0.0)
    block = lax.psum(jnp.dot(place, own_rows, precision=highest), ("rows", "cols"))
    lower = jnp.linalg.cholesky(block)
    full = jax.scipy.linalg.solve_triangular(lower, panel.T, lower=True).T
    facf = factor_cols.astype(jnp.float32)
    gains = row_q * row_q + RIDGE - jnp.sum(facf * facf, axis=1) - jnp.sum(full * full, axis=1)
    best = lax.pmax(jnp.max(gains), ("rows", "cols"))
    return (full.astype(jnp.bfloat16), gains, best)


def solution(mesh):
    in_specs = (P(("rows", "cols"), None), P(("rows", "cols"), None), P(("rows", "cols")), P())
    out_specs = (P(("rows", "cols"), None), P(("rows", "cols")), P())
    return jax.shard_map(body, mesh=mesh, in_specs=in_specs, out_specs=out_specs, check_vma=False)
```

profile of v0, /device:TPU:1, one launch (start us, length us, event | category | flops | bytes accessed | tf_op | source)
XLA Modules:
  0.0 518.1 jit_solution(16837783540909877693)
XLA Ops:
  7.2 1.3 fusion.28
  9.2 1.3 gather_fusion
  11.2 4.6 gather_fusion.5
  16.6 7.7 %gather_fusion.3 = bf16[16,1024]{1,0:T(8,128)(2,1)S(1)} fusion(bf16[7168,1024]{1,0:T(8,128)(2,1)} %param.4, s32[1024]{0:T(1024)S(1)} %pad_clamp_fusion.1), kind=kCustom, calls=%fused_computation.3 | custom fusion | bytes 65600 | tf_op jit(solution)/shard_map/gather | solution.py:48
  25.0 1.4 gather_fusion.1
  27.3 69.2 %all-reduce.1 = bf16[2048]{0:T(1024)(128)(2,1)S(1)} all-reduce(bf16[2048]{0:T(1024)(128)(2,1)S(1)} %dynamic-update-slice.11), channel_id=1, replica_groups=mesh['rows'=8,'cols'=16] {'rows','cols'}, use_global_device_ids=true, to_apply=%add.1 | all-reduce | flops 2048 | bytes 8192
  96.8 1.9 gather_fusion.2
  99.3 8.1 %multiply_reduce_fusion = f32[7168]{0:T(1024)S(1)} fusion(bf16[7168,1024]{1,0:T(8,128)(2,1)} %param.4), kind=kLoop, calls=%fused_computation.10 | loop fusion | flops 22012928 | bytes 14708736 | tf_op jit(solution)/shard_map/reduce_sum | solution.py:19
  107.5 3.1 gather_fusion.6
  110.6 42.8 %all-gather.3.cloned.1.call-done = bf16[2048,1024]{1,0:T(8,128)(2,1)} async-done(((bf16[16,1024]{1,0:T(8,128)(2,1)}), bf16[2048,1024]{1,0:T(8,128)(2,1)}) %all-gather.3.cloned.1.call-update) | async-done | bytes 4194320 | tf_op jit(solution)/shard_map/all_gather | solution.py:56
  153.4 4.3 gather_fusion.4
  157.7 16.8 %fusion.34 = f32[256,7168]{1,0:T(8,128)} fusion(bf16[256,1024]{1,0:T(8,128)(2,1)S(1)} %gather_fusion.4, bf16[7168,1024]{1,0:T(8,128)(2,1)} %param.4), kind=kOutput, calls=%fused_computation.90 | convolution fusion | flops 3758096384 | bytes 22544384 | tf_op jit(solution)/shard_map/dot_general | solution.py:26
  174.7 25.6 %add_subtract_fusion = (f32[256,7168]{1,0:T(8,128)}, f32[256,7168]{1,0:T(8,128)}) fusion(f32[256,7168]{1,0:T(8,128)} %fusion.34, s32[7168]{0:T(1024)S(1)} %iota_add_fusion, f32[256]{0:T(256)S(1)} %add_sqrt_fusion, f32[7168]{0:T(1024)S(1)} %get-tuple-element.44, f32[256]{0:T(256)S(1)} %fusion.26, f32[7168]{0:T(1024)S(1)} %get-tuple-element.43, ...), kind=kOutput, calls=%fused_computation.22 | convolution fusion | flops 1897398272 | bytes 29711360 | tf_op jit(solution)/shard_map/dot_general | solution.py:31
  200.3 7.2 %bitcast_subtract_fusion = f32[7168,256]{0,1:T(8,128)} fusion(f32[256,7168]{1,0:T(8,128)} %get-tuple-element.40, f32[256,7168]{1,0:T(8,128)S(1)} %bitcast.60, s32[7168]{0:T(1024)S(1)} %iota_add_fusion, f32[256]{0:T(256)S(1)} %add_sqrt_fusion, f32[7168]{0:T(1024)S(1)} %get-tuple-element.44, f32[256]{0:T(256)S(1)} %fusion.26, f32[7168]{0:T(1024)S(1)} %get-tuple-element.43, ...), kind=kLoop, calls=%fused_computation.14 | loop fusion | flops 18350080 | bytes 22109184 | tf_op jit(solution)/shard_map/sub | solution.py:32
  207.6 8.4 %copy.15 = f32[7168,256]{1,0:T(8,128)} copy(f32[7168,256]{0,1:T(8,128)} %bitcast_subtract_fusion) | data formatting | bytes 14680064 | tf_op jit(solution)/shard_map/sub | solution.py:32
  215.9 3.7 gather_fusion.7
  220.7 4.6 multiply_reduce_fusion.1
  225.3 135.9 %all-reduce.4.cloned.1.call-done = f32[256,256]{0,1:T(8,128)} async-done(((f32[256,256]{0,1:T(8,128)}), f32[256,256]{0,1:T(8,128)}) %all-reduce.4.cloned.1.call-update) | async-done | bytes 262160 | tf_op jit(solution)/shard_map/psum | solution.py:82
  363.3 11.7 %cholesky.50 = f32[128,128]{1,0:T(8,128)S(1)} custom-call(f32[128,128]{1,0:T(8,128)S(1)} %cholesky.118), custom_call_target="Cholesky" | custom-call | tf_op jit(solution)/shard_map/jit(cholesky)/cholesky | solution.py:83
  375.1 9.8 %custom-call.15 = f32[1,128,128]{1,2,0:T(8,128)S(1)} custom-call(f32[1,128,128]{2,1,0:T(8,128)S(1)} %get-tuple-element.38), custom_call_target="InvertDiagBlocksLowerTriangular" | custom-call | tf_op jit(solution)/shard_map/jit(cholesky)/cholesky | solution.py:83
  385.4 11.7 %cholesky.105 = f32[128,128]{1,0:T(8,128)S(1)} custom-call(f32[128,128]{1,0:T(8,128)S(1)} %convolution_subtract_fusion.1), custom_call_target="Cholesky" | custom-call | tf_op jit(solution)/shard_map/jit(cholesky)/cholesky | solution.py:83
  399.8 4.0 while.1
  400.4 1.4 bitcast_dynamic-update-slice_fusion.2
  402.4 1.4 bitcast_dynamic-update-slice_fusion.2
  403.8 19.9 %custom-call.16 = f32[2,128,128]{1,2,0:T(8,128)S(1)} custom-call(f32[2,128,128]{2,1,0:T(8,128)S(1)} %get-tuple-element.10), custom_call_target="InvertDiagBlocksLowerTriangular" | custom-call | tf_op jit(solution)/shard_map/jit(_solve_triangular)/triangular_solve | solution.py:84
  423.7 5.5 %fusion.7 = f32[128,7168]{1,0:T(8,128)S(1)} fusion(f32[256,7168]{1,0:T(8,128)} %get-tuple-element.39, f32[2,128,128]{1,2,0:T(8,128)S(1)} %custom-call.16), kind=kOutput, calls=%fused_computation.25 | convolution fusion | flops 1409286144 | bytes 7405568 | tf_op jit(solution)/shard_map/jit(_solve_triangular)/triangular_solve | solution.py:84
  429.2 5.3 %convolution_subtract_fusion = f32[128,7168]{1,0:T(8,128)S(1)} fusion(f32[128,7168]{1,0:T(8,128)S(1)} %fusion.7, f32[256,7168]{1,0:T(8,128)} %get-tuple-element.39, f32[256,256]{1,0:T(8,128)S(1)} %get-tuple-element.94), kind=kOutput, calls=%fused_computation.12 | convolution fusion | flops 1410203648 | bytes 11075584 | tf_op jit(solution)/shard_map/jit(_solve_triangular)/triangular_solve | solution.py:84
  434.5 3.5 fusion.14
  438.6 2.3 fusion.6
  440.9 1.2 fusion.32
  442.1 63.3 %pmax.7 = f32[]{:T(128)} all-reduce(f32[]{:T(128)} %get-tuple-element.30), channel_id=1, replica_groups=mesh['rows'=8,'cols'=16] {'rows','cols'}, use_global_device_ids=true, to_apply=%region_13.14 | all-reduce | flops 1 | bytes 8 | tf_op jit(solution)/shard_map/pmax | solution.py:87
  505.4 5.9 %copy.18 = bf16[7168,256]{1,0:T(8,128)(2,1)} copy(bf16[7168,256]{0,1:T(8,128)(2,1)} %fusion.6) | data formatting | bytes 7340032
  (55 shorter events, 11.7 us)
Async XLA Ops:
  7.2 100.4 %all-gather.5.cloned.1.call-start = ((), (), s32[]{:S(2)}) async-start(), calls=%async_computation.1 | async-start | bytes 2113536 | tf_op jit(solution)/shard_map/all_gather | solution.py:57
  16.5 136.8 %all-gather.3.cloned.1.call-start = ((), (), s32[]{:S(2)}) async-start(), calls=%async_computation | async-start | bytes 4227072 | tf_op jit(solution)/shard_map/all_gather | solution.py:56
  25.0 336.2 %all-reduce.4.cloned.1.call-start = ((), (), s32[]{:S(2)}) async-start(), calls=%async_computation.2 | async-start | bytes 524288 | tf_op jit(solution)/shard_map/psum | solution.py:82
  99.3 8.1 %copy-start.1 = (s32[7168]{0:T(1024)S(1)}, s32[7168]{0:T(1024)}, u32[]{:S(2)}) copy-start(s32[7168]{0:T(1024)} %param.6) | copy-start | bytes 86020
  157.7 17.0 %copy-start = (s32[256]{0:T(256)S(1)}, s32[256]{0:T(256)}, u32[]{:S(2)}) copy-start(s32[256]{0:T(256)} %param.7) | copy-start | bytes 3076
  174.5 25.9 %slice-start = ((s8[7340032]{0:T(1024)(128)(4,1)}), s8[4194304]{0:T(1024)(128)(4,1)S(1)}, s32[]{:S(2)}) async-start(s8[7340032]{0:T(1024)(128)(4,1)} %bitcast.59), calls=%async_computation.3 | async-start | bytes 8388608
  174.7 25.7 %slice-start.1 = ((s8[7340032]{0:T(1024)(128)(4,1)}), s8[3145728]{0:T(1024)(128)(4,1)S(1)}, s32[]{:S(2)}) async-start(s8[7340032]{0:T(1024)(128)(4,1)} %bitcast.59), calls=%async_computation.4 | async-start | bytes 6291456
Sparse Core Ops, SparseCore 0:
  16.6 69.0 all-gather.4
  89.4 63.9 all-gather.2
  220.8 140.3 all-reduce.3
where the time goes:
time: 522 us; the launch traced here: 518 us
  waiting for transfers between devices  179 us (34%)
  blocking collectives  133 us (25%)
  other arithmetic  85.1 us (16%)
  matrix products  58.3 us (11%)
  local copies, waits for them, and re-layouts  47.7 us (9%)
  between operations  15.6 us (3%)
    psum x1, waiting for transfers between devices, body(): lax.psum(jnp.dot(place, own_rows, precision=highest), ('rows', 'cols'))  136 us
    unnamed x1, blocking collectives  69.2 us
    pmax x1, blocking collectives, body(): best = lax.pmax(jnp.max(gains), ('rows', 'cols'))  63.3 us
    all_gather x1, waiting for transfers between devices, body(): lax.all_gather(own_emb, ('rows', 'cols'), axis=0, tiled=True)  42.8 us
    another operation x7, other arithmetic, body(): lower = jnp.linalg.cholesky(block)  34.6 us
    dot_general x1, matrix products, kernel_panel(): lax.dot_general(left_fac, piv_fac, dims, preferred_element_type=jnp.float32)  25.6 us
    another operation x3, other arithmetic, body(): full = jax.scipy.linalg.solve_triangular(lower, panel.T, lower=True).T  19.9 us
    dot_general x1, matrix products, kernel_panel(): lax.dot_general(left_emb, piv_emb, dims, preferred_element_type=jnp.float32)  16.8 us
  transfers between devices with their start and end apart: 3, of which 2 were waited for; matrix products, arithmetic and copies ran while one was open for 6% of the time, Pallas kernels for 0%

commit v1 on v0

--- a/solution.py
+++ b/solution.py
@@ -79,7 +79,9 @@
         pivots,
     )
     own_rows = jnp.where(keep, panel[local_idx], 0.0)
-    block = lax.psum(jnp.dot(place, own_rows, precision=highest), ("rows", "cols"))
+    block = jnp.sum(
+        lax.all_gather(jnp.dot(place, own_rows, precision=highest), ("rows", "cols")), axis=0
+    )
     lower = jnp.linalg.cholesky(block)
     full = jax.scipy.linalg.solve_triangular(lower, panel.T, lower=True).T
     facf = factor_cols.astype(jnp.float32)

time: 522 us -> 486 us (0.931)
  waiting for transfers between devices: 179 us -> 142 us
  matrix products: 58.3 us -> 46.5 us
  other arithmetic: 85.1 us -> 96.4 us
    psum x1 -> x0, waiting for transfers between devices: 136 us -> none  [body(): lax.psum(jnp.dot(place, own_rows, precision=highest), ('rows', 'cols'))]
    all_gather x0 -> x1, waiting for transfers between devices: none -> 99.5 us  [body(): lax.all_gather(jnp.dot(place, own_rows, precision=highest), ('rows', 'col...]
    dot_general x1, matrix products: 25.6 us -> 13.5 us  [kernel_panel(): lax.dot_general(left_fac, piv_fac, dims, preferred_element_type=jnp.float32)]
    reduce_sum x0 -> x1, other arithmetic: none -> 12.1 us  [body(): jnp.sum(lax.all_gather(jnp.dot(place, own_rows, precision=highest), ('row...]
where the time goes in v1:
time: 486 us; the launch traced here: 481 us
  waiting for transfers between devices  142 us (29%)
  blocking collectives  134 us (28%)
  other arithmetic  96.4 us (20%)
  local copies, waits for them, and re-layouts  46.7 us (10%)
  matrix products  46.5 us (10%)
  between operations  15.6 us (3%)
    all_gather x1, waiting for transfers between devices, body(): lax.all_gather(jnp.dot(place, own_rows, precision=highest), ('rows', 'col...  99.5 us
    unnamed x1, blocking collectives  69.1 us
    pmax x1, blocking collectives, body(): best = lax.pmax(jnp.max(gains), ('rows', 'cols'))  64.5 us
    all_gather x1, waiting for transfers between devices, body(): lax.all_gather(own_emb, ('rows', 'cols'), axis=0, tiled=True)  42.9 us
    another operation x7, other arithmetic, body(): lower = jnp.linalg.cholesky(block)  34.6 us
    another operation x3, other arithmetic, body(): full = jax.scipy.linalg.solve_triangular(lower, panel.T, lower=True).T  19.9 us
    dot_general x1, matrix products, kernel_panel(): lax.dot_general(left_emb, piv_emb, dims, preferred_element_type=jnp.float32)  16.9 us
    another operation x3, matrix products, body(): full = jax.scipy.linalg.solve_triangular(lower, panel.T, lower=True).T  14.6 us
  transfers between devices with their start and end apart: 3, of which 2 were waited for; matrix products, arithmetic and copies ran while one was open for 6% of the time, Pallas kernels for 0%

profile of v1, /device:TPU:1, one launch (start us, length us, event | category | flops | bytes accessed | tf_op | source)
XLA Modules:
  0.0 481.4 jit_solution(9502996314257893807)
XLA Ops:
  7.2 1.3 fusion.28
  9.2 1.3 gather_fusion
  11.2 4.6 gather_fusion.5
  16.6 7.7 %gather_fusion.3 = bf16[16,1024]{1,0:T(8,128)(2,1)S(1)} fusion(bf16[7168,1024]{1,0:T(8,128)(2,1)} %param.4, s32[1024]{0:T(1024)S(1)} %pad_clamp_fusion.1), kind=kCustom, calls=%fused_computation.3 | custom fusion | bytes 65600 | tf_op jit(solution)/shard_map/gather | solution.py:48
  25.0 1.4 gather_fusion.1
  27.3 69.1 %all-reduce.1 = bf16[2048]{0:T(1024)(128)(2,1)S(1)} all-reduce(bf16[2048]{0:T(1024)(128)(2,1)S(1)} %dynamic-update-slice.11), channel_id=1, replica_groups=mesh['rows'=8,'cols'=16] {'rows','cols'}, use_global_device_ids=true, to_apply=%add.1 | all-reduce | flops 2048 | bytes 8192
  96.7 1.9 gather_fusion.2
  99.2 8.1 %multiply_reduce_fusion = f32[7168]{0:T(1024)S(1)} fusion(bf16[7168,1024]{1,0:T(8,128)(2,1)} %param.4), kind=kLoop, calls=%fused_computation.10 | loop fusion | flops 22012928 | bytes 14708736 | tf_op jit(solution)/shard_map/reduce_sum | solution.py:19
  107.4 3.1 gather_fusion.6
  110.5 42.9 %all-gather.5.cloned.1.call-done = bf16[2048,1024]{1,0:T(8,128)(2,1)} async-done(((bf16[16,1024]{1,0:T(8,128)(2,1)}), bf16[2048,1024]{1,0:T(8,128)(2,1)}) %all-gather.5.cloned.1.call-update) | async-done | bytes 4194320 | tf_op jit(solution)/shard_map/all_gather | solution.py:56
  153.4 4.3 gather_fusion.4
  157.7 16.9 %fusion.34 = f32[256,7168]{1,0:T(8,128)} fusion(bf16[256,1024]{1,0:T(8,128)(2,1)S(1)} %gather_fusion.4, bf16[7168,1024]{1,0:T(8,128)(2,1)} %param.4), kind=kOutput, calls=%fused_computation.90 | convolution fusion | flops 3758096384 | bytes 22544384 | tf_op jit(solution)/shard_map/dot_general | solution.py:26
  174.8 13.5 %add_subtract_fusion = (f32[256,7168]{1,0:T(8,128)}, f32[256,7168]{1,0:T(8,128)}) fusion(f32[256,7168]{1,0:T(8,128)} %fusion.34, s32[7168]{0:T(1024)S(1)} %iota_add_fusion, f32[256]{0:T(256)S(1)} %add_sqrt_fusion, f32[7168]{0:T(1024)S(1)} %get-tuple-element.47, f32[256]{0:T(256)S(1)} %fusion.26, f32[7168]{0:T(1024)S(1)} %get-tuple-element.46, ...), kind=kOutput, calls=%fused_computation.22 | convolution fusion | flops 1897398272 | bytes 29711360 | tf_op jit(solution)/shard_map/dot_general | solution.py:31
  188.3 7.3 %bitcast_subtract_fusion = f32[7168,256]{0,1:T(8,128)} fusion(f32[256,7168]{1,0:T(8,128)} %get-tuple-element.43, f32[256,7168]{1,0:T(8,128)S(1)} %bitcast.62, s32[7168]{0:T(1024)S(1)} %iota_add_fusion, f32[256]{0:T(256)S(1)} %add_sqrt_fusion, f32[7168]{0:T(1024)S(1)} %get-tuple-element.47, f32[256]{0:T(256)S(1)} %fusion.26, f32[7168]{0:T(1024)S(1)} %get-tuple-element.46, ...), kind=kLoop, calls=%fused_computation.14 | loop fusion | flops 18350080 | bytes 22109184 | tf_op jit(solution)/shard_map/sub | solution.py:32
  195.6 8.4 %copy.16 = f32[7168,256]{1,0:T(8,128)} copy(f32[7168,256]{0,1:T(8,128)} %bitcast_subtract_fusion) | data formatting | bytes 14680064 | tf_op jit(solution)/shard_map/sub | solution.py:32
  204.0 3.7 gather_fusion.7
  208.7 4.6 multiply_reduce_fusion.1
  213.3 99.5 %all-gather.9.cloned.1.call-done = f32[32768,256]{1,0:T(8,128)} async-done(((f32[256,256]{1,0:T(8,128)}), f32[32768,256]{1,0:T(8,128)}) %all-gather.9.cloned.1.call-update) | async-done | bytes 33554448 | tf_op jit(solution)/shard_map/all_gather | solution.py:83
  312.8 12.1 %reduce_sum.77 = f32[256,256]{1,0:T(8,128)S(1)} reduce(f32[128,256,256]{2,1,0:T(8,128)} %bitcast.60, f32[]{:T(128)} %constant.136.clone.1), dimensions={0}, to_apply=%region_5.6 | reduce | flops 8323072 | bytes 33816580 | tf_op jit(solution)/shard_map/reduce_sum | solution.py:82
  325.1 11.7 %cholesky.50 = f32[128,128]{1,0:T(8,128)S(1)} custom-call(f32[128,128]{1,0:T(8,128)S(1)} %cholesky.118), custom_call_target="Cholesky" | custom-call | tf_op jit(solution)/shard_map/jit(cholesky)/cholesky | solution.py:85
  336.9 9.8 %custom-call.15 = f32[1,128,128]{1,2,0:T(8,128)S(1)} custom-call(f32[1,128,128]{2,1,0:T(8,128)S(1)} %get-tuple-element.41), custom_call_target="InvertDiagBlocksLowerTriangular" | custom-call | tf_op jit(solution)/shard_map/jit(cholesky)/cholesky | solution.py:85
  347.2 11.7 %cholesky.105 = f32[128,128]{1,0:T(8,128)S(1)} custom-call(f32[128,128]{1,0:T(8,128)S(1)} %convolution_subtract_fusion.1), custom_call_target="Cholesky" | custom-call | tf_op jit(solution)/shard_map/jit(cholesky)/cholesky | solution.py:85
  361.6 4.0 while.1
  362.2 1.4 bitcast_dynamic-update-slice_fusion.2
  364.2 1.4 bitcast_dynamic-update-slice_fusion.2
  365.6 19.9 %custom-call.16 = f32[2,128,128]{1,2,0:T(8,128)S(1)} custom-call(f32[2,128,128]{2,1,0:T(8,128)S(1)} %get-tuple-element.10), custom_call_target="InvertDiagBlocksLowerTriangular" | custom-call | tf_op jit(solution)/shard_map/jit(_solve_triangular)/triangular_solve | solution.py:86
  385.5 5.5 %fusion.7 = f32[128,7168]{1,0:T(8,128)S(1)} fusion(f32[256,7168]{1,0:T(8,128)} %get-tuple-element.42, f32[2,128,128]{1,2,0:T(8,128)S(1)} %custom-call.16), kind=kOutput, calls=%fused_computation.25 | convolution fusion | flops 1409286144 | bytes 7405568 | tf_op jit(solution)/shard_map/jit(_solve_triangular)/triangular_solve | solution.py:86
  391.0 5.6 %convolution_subtract_fusion = f32[128,7168]{1,0:T(8,128)S(1)} fusion(f32[128,7168]{1,0:T(8,128)S(1)} %fusion.7, f32[256,7168]{1,0:T(8,128)} %get-tuple-element.42, f32[256,256]{1,0:T(8,128)S(1)} %get-tuple-element.98), kind=kOutput, calls=%fused_computation.12 | convolution fusion | flops 1410203648 | bytes 11075584 | tf_op jit(solution)/shard_map/jit(_solve_triangular)/triangular_solve | solution.py:86
  396.6 3.5 fusion.14
  400.8 2.3 fusion.6
  404.3 64.5 %pmax.7 = f32[]{:T(128)} all-reduce(f32[]{:T(128)} %get-tuple-element.33), channel_id=1, replica_groups=mesh['rows'=8,'cols'=16] {'rows','cols'}, use_global_device_ids=true, to_apply=%region_13.14 | all-reduce | flops 1 | bytes 8 | tf_op jit(solution)/shard_map/pmax | solution.py:89
  468.7 5.9 %copy.18 = bf16[7168,256]{1,0:T(8,128)(2,1)} copy(bf16[7168,256]{0,1:T(8,128)(2,1)} %fusion.6) | data formatting | bytes 7340032
  (56 shorter events, 10.9 us)
Async XLA Ops:
  7.2 100.3 %all-gather.7.cloned.1.call-start = ((), (), s32[]{:S(2)}) async-start(), calls=%async_computation.1 | async-start | bytes 2113536 | tf_op jit(solution)/shard_map/all_gather | solution.py:57
  16.5 136.9 %all-gather.5.cloned.1.call-start = ((), (), s32[]{:S(2)}) async-start(), calls=%async_computation | async-start | bytes 4227072 | tf_op jit(solution)/shard_map/all_gather | solution.py:56
  25.0 287.8 %all-gather.9.cloned.1.call-start = ((), (), s32[]{:S(2)}) async-start(), calls=%async_computation.2 | async-start | bytes 33816576 | tf_op jit(solution)/shard_map/all_gather | solution.py:83
  99.2 8.1 %copy-start.1 = (s32[7168]{0:T(1024)S(1)}, s32[7168]{0:T(1024)}, u32[]{:S(2)}) copy-start(s32[7168]{0:T(1024)} %param.6) | copy-start | bytes 86020
  157.7 17.1 %copy-start = (s32[256]{0:T(256)S(1)}, s32[256]{0:T(256)}, u32[]{:S(2)}) copy-start(s32[256]{0:T(256)} %param.7) | copy-start | bytes 3076
  174.5 13.7 %slice-start = ((s8[7340032]{0:T(1024)(128)(4,1)}), s8[4194304]{0:T(1024)(128)(4,1)S(1)}, s32[]{:S(2)}) async-start(s8[7340032]{0:T(1024)(128)(4,1)} %bitcast.61), calls=%async_computation.3 | async-start | bytes 8388608
  174.7 13.5 %slice-start.1 = ((s8[7340032]{0:T(1024)(128)(4,1)}), s8[3145728]{0:T(1024)(128)(4,1)S(1)}, s32[]{:S(2)}) async-start(s8[7340032]{0:T(1024)(128)(4,1)} %bitcast.61), calls=%async_computation.4 | async-start | bytes 6291456
Sparse Core Ops, SparseCore 0:
  16.6 69.0 all-gather.6
  89.4 63.9 all-gather.4
  208.8 103.9 all-gather.8
